TPU v7x, 32 devices: a whole 2x2x4 slice. The times are simulated.
32 devices in a mesh: dp: 8 (over z, x), seq: 4 (over y, core).
Axes of the slice: x: 2, y: 2, z: 4, core: 2. Of those that a mesh axis runs over, the one named last changes fastest.
Arguments:
- tokens: bfloat16 [16384, 1024], P(('dp', 'seq')), may hold values from -6 to 6
- time_embed: bfloat16 [32, 1024], P(('dp', 'seq')), may hold values from -6 to 6
- lengths: int32 [32], P('dp'), may hold values from 0 to 475, as said below
- cotangent: bfloat16 [16384, 1024], P(('dp', 'seq')), may hold values from -6 to 6
- w_query: bfloat16 [1024, 1024], P('seq'), may hold values from -0.1875 to 0.1875
- w_key: bfloat16 [1024, 1024], P('seq'), may hold values from -0.1875 to 0.1875
- w_value: bfloat16 [1024, 1024], P('seq'), may hold values from -0.1875 to 0.1875
- w_out: bfloat16 [1024, 1024], P('seq'), may hold values from -0.75 to 0.75
- w_time: bfloat16 [1024, 1024], P('seq'), may hold values from -0.1875 to 0.1875
- w_in: bfloat16 [4096, 1024], P('seq'), may hold values from -0.1875 to 0.1875
- w_down: bfloat16 [4096, 1024], P('seq'), may hold values from -0.09375 to 0.09375
- b_query: bfloat16 [1024], replicated, may hold values from -3 to 3
- b_value: bfloat16 [1024], replicated, may hold values from -3 to 3
- b_out: bfloat16 [1024], replicated, may hold values from -3 to 3
- b_time: bfloat16 [1024], replicated, may hold values from -3 to 3
- b_in: bfloat16 [4096], replicated, may hold values from -3 to 3
- b_down: bfloat16 [1024], replicated, may hold values from -2 to 2
- gain_one: bfloat16 [1024], replicated, may hold values from 0.25 to 1.75
- shift_one: bfloat16 [1024], replicated, may hold values from -2 to 2
- gain_two: bfloat16 [1024], replicated, may hold values from 0.25 to 1.75
- shift_two: bfloat16 [1024], replicated, may hold values from -2 to 2
Outputs:
- layer_out: bfloat16 [16384, 1024], P(('dp', 'seq'))
- grad_tokens: bfloat16 [16384, 1024], P(('dp', 'seq'))
- grad_w_query: float32 [1024, 1024], P('seq')
- grad_w_key: float32 [1024, 1024], P('seq')
- grad_w_value: float32 [1024, 1024], P('seq')
- grad_w_out: float32 [1024, 1024], P('seq')
- grad_w_time: float32 [1024, 1024], P('seq')
- grad_w_in: float32 [4096, 1024], P('seq')
- grad_w_down: float32 [4096, 1024], P('seq')
- grad_b_query: float32 [1024], replicated
- grad_b_value: float32 [1024], replicated
- grad_b_out: float32 [1024], replicated
- grad_b_time: float32 [1024], replicated
- grad_b_in: float32 [4096], replicated
- grad_b_down: float32 [1024], replicated
- grad_gain_one: float32 [1024], replicated
- grad_shift_one: float32 [1024], replicated
- grad_gain_two: float32 [1024], replicated
- grad_shift_two: float32 [1024], replicated
Inputs may be any that keep to these rules, and one draw needn't show every extreme that they name: Item i's valid slots are its first lengths[i] + 25; every draw has an item of length 475 and one of length 0.
All inputs are finite; a program needn't handle non-finite values.
Results may differ from a plain program's by a relative error of at most 0.02.
Values may be sent and summed in bfloat16 or wider, within the bound.
A program may use at most 256 MiB of HBM per device.

v0:
```python
import jax
import jax.numpy as jnp
from jax import lax
from jax.sharding import PartitionSpec as P

HEAD_DIM = 64
BLOCK = 25
norm_eps = 1e-05
neg_large = -1e30


def layer_norm(values, gain, shift):
    center = values - jnp.mean(values, axis=-1, keepdims=True)
    spread = lax.rsqrt(jnp.mean(center * center, axis=-1, keepdims=True) + norm_eps)
    return center * spread * gain + shift


def exact_gelu(values):
    return jax.nn.gelu(values, approximate=False)


def split_heads(rows):
    return rows.reshape(rows.shape[0], rows.shape[1] // HEAD_DIM, HEAD_DIM)


def item_scores(item_block, key_valid):
    queries = split_heads(item_block[:, 0])
    key_heads = split_heads(item_block[:, 1])
    value_heads = split_heads(item_block[:, 2])
    scores = jnp.einsum(
        "qhd,khd->hqk", queries, key_heads, preferred_element_type=jnp.float32
    ) * HEAD_DIM ** (-0.5)
    masked = jnp.where(key_valid[None, None, :], scores, neg_large)
    return (queries, key_heads, value_heads, masked)


def attend_forward(packed):
    item_block, key_valid = packed
    queries, key_heads, value_heads, masked = item_scores(item_block, key_valid)
    row_max = jnp.max(masked, axis=-1, keepdims=True)
    exp_scores = jnp.exp(masked - row_max)
    row_total = jnp.sum(exp_scores, axis=-1, keepdims=True)
    soft_weights = (exp_scores / row_total).astype(jnp.bfloat16)
    mixed_heads = jnp.einsum(
        "hqk,khd->qhd", soft_weights, value_heads, preferred_element_type=jnp.float32
    )
    log_total = row_max[:, :, 0] + jnp.log(row_total[:, :, 0])
    return (mixed_heads.reshape(item_block.shape[0], -1).astype(jnp.bfloat16), log_total)


def attend_backward(packed):
    item_block, key_valid, log_total, grad_block = packed
    queries, key_heads, value_heads, masked = item_scores(item_block, key_valid)
    soft_weights = jnp.exp(masked - log_total[:, :, None])
    grad_heads = split_heads(grad_block)
    grad_value = jnp.einsum(
        "hqk,qhd->khd",
        soft_weights.astype(jnp.bfloat16),
        grad_heads,
        preferred_element_type=jnp.float32,
    )
    grad_soft = jnp.einsum(
        "qhd,khd->hqk", grad_heads, value_heads, preferred_element_type=jnp.float32
    )
    grad_scores = soft_weights * (
        grad_soft - jnp.sum(soft_weights * grad_soft, axis=-1, keepdims=True)
    )
    scores_low = grad_scores.astype(jnp.bfloat16)
    score_scale = HEAD_DIM ** (-0.5)
    grad_query = (
        jnp.einsum("hqk,khd->qhd", scores_low, key_heads, preferred_element_type=jnp.float32)
        * score_scale
    )
    grad_key = (
        jnp.einsum("hqk,qhd->khd", scores_low, queries, preferred_element_type=jnp.float32)
        * score_scale
    )
    slot_count = item_block.shape[0]
    return jnp.stack(
        [
            grad_query.reshape(slot_count, -1),
            grad_key.reshape(slot_count, -1),
            grad_value.reshape(slot_count, -1),
        ],
        axis=1,
    ).astype(jnp.bfloat16)


def local(
    tokens,
    time_embed,
    lengths,
    cotangent,
    w_query,
    w_key,
    w_value,
    w_out,
    w_time,
    w_in,
    w_down,
    b_query,
    b_value,
    b_out,
    b_time,
    b_in,
    b_down,
    gain_one,
    shift_one,
    gain_two,
    shift_two,
):
    seq_rank = lax.axis_index("seq")
    item_count = time_embed.shape[0]
    token_count = tokens.shape[0]
    slot_count = token_count // item_count
    model_width = tokens.shape[1]
    full_query, full_key, full_value, full_out, full_time, full_in, full_down = (
        lax.all_gather(w_query, "seq", axis=0, tiled=True),
        lax.all_gather(w_key, "seq", axis=0, tiled=True),
        lax.all_gather(w_value, "seq", axis=0, tiled=True),
        lax.all_gather(w_out, "seq", axis=0, tiled=True),
        lax.all_gather(w_time, "seq", axis=0, tiled=True),
        lax.all_gather(w_in, "seq", axis=0, tiled=True),
        lax.all_gather(w_down, "seq", axis=0, tiled=True),
    )
    bias_query = b_query.astype(jnp.float32)
    bias_value = b_value.astype(jnp.float32)
    bias_out = b_out.astype(jnp.float32)
    bias_time = b_time.astype(jnp.float32)
    bias_in = b_in.astype(jnp.float32)
    bias_down = b_down.astype(jnp.float32)
    gain_first = gain_one.astype(jnp.float32)
    shift_first = shift_one.astype(jnp.float32)
    gain_last = gain_two.astype(jnp.float32)
    shift_last = shift_two.astype(jnp.float32)
    slot_index = lax.broadcasted_iota(jnp.int32, (lengths.shape[0], slot_count), 1)
    group_valid = slot_index < lengths[:, None] + BLOCK
    own_valid = lax.dynamic_slice_in_dim(group_valid, seq_rank * item_count, item_count, 0)
    row_keep = own_valid.reshape(token_count, 1).astype(jnp.float32)
    time_proj = jnp.dot(time_embed, full_time, preferred_element_type=jnp.float32) + bias_time
    resid = (tokens.reshape(item_count, slot_count, model_width) + time_proj[:, None, :]).reshape(
        token_count, model_width
    )
    resid_low = resid.astype(jnp.bfloat16)
    query_rows = (
        jnp.dot(resid_low, full_query, preferred_element_type=jnp.float32) + bias_query
    ).astype(jnp.bfloat16)
    key_rows = jnp.dot(resid_low, full_key, preferred_element_type=jnp.float32).astype(jnp.bfloat16)
    value_rows = (
        jnp.dot(resid_low, full_value, preferred_element_type=jnp.float32) + bias_value
    ).astype(jnp.bfloat16)
    stacked = jnp.stack([query_rows, key_rows, value_rows], axis=1).reshape(
        item_count, slot_count, 3, model_width
    )
    head_side = lax.all_to_all(stacked, "seq", split_axis=3, concat_axis=0, tiled=True)
    mixed_heads, log_totals = lax.map(attend_forward, (head_side, group_valid))
    mixed_rows = lax.all_to_all(
        mixed_heads, "seq", split_axis=0, concat_axis=2, tiled=True
    ).reshape(token_count, model_width)
    attn_out = jnp.dot(mixed_rows, full_out, preferred_element_type=jnp.float32) + bias_out
    first_norm, first_pull = jax.vjp(layer_norm, resid + attn_out, gain_first, shift_first)
    first_low = first_norm.astype(jnp.bfloat16)
    hidden_pre = (
        jnp.einsum("td,fd->tf", first_low, full_in, preferred_element_type=jnp.float32) + bias_in
    )
    hidden, gelu_pull = jax.vjp(exact_gelu, hidden_pre)
    hidden_low = hidden.astype(jnp.bfloat16)
    ffn_out = jnp.dot(hidden_low, full_down, preferred_element_type=jnp.float32) + bias_down
    second_norm, second_pull = jax.vjp(layer_norm, first_norm + ffn_out, gain_last, shift_last)
    layer_out = (second_norm * row_keep).astype(jnp.bfloat16)
    back_query, back_key, back_value, back_out, back_in, back_down = (
        lax.all_gather(w_query, "seq", axis=0, tiled=True),
        lax.all_gather(w_key, "seq", axis=0, tiled=True),
        lax.all_gather(w_value, "seq", axis=0, tiled=True),
        lax.all_gather(w_out, "seq", axis=0, tiled=True),
        lax.all_gather(w_in, "seq", axis=0, tiled=True),
        lax.all_gather(w_down, "seq", axis=0, tiled=True),
    )
    grad_second_in, grad_gain_two, grad_shift_two = second_pull(
        cotangent.astype(jnp.float32) * row_keep
    )
    grad_ffn = grad_second_in.astype(jnp.bfloat16)
    grad_hidden = jnp.einsum("td,fd->tf", grad_ffn, back_down, preferred_element_type=jnp.float32)
    grad_pre = gelu_pull(grad_hidden)[0].astype(jnp.bfloat16)
    grad_first = grad_second_in + jnp.dot(grad_pre, back_in, preferred_element_type=jnp.float32)
    grad_first_in, grad_gain_one, grad_shift_one = first_pull(grad_first)
    grad_attn = grad_first_in.astype(jnp.bfloat16)
    grad_mixed = jnp.einsum(
        "td,ed->te", grad_attn, back_out, preferred_element_type=jnp.float32
    ).astype(jnp.bfloat16)
    grad_heads = lax.all_to_all(
        grad_mixed.reshape(item_count, slot_count, model_width),
        "seq",
        split_axis=2,
        concat_axis=0,
        tiled=True,
    )
    grad_stack = lax.map(attend_backward, (head_side, group_valid, log_totals, grad_heads))
    grad_qkv = lax.all_to_all(grad_stack, "seq", split_axis=0, concat_axis=3, tiled=True).reshape(
        token_count, 3, model_width
    )
    grad_query_rows = grad_qkv[:, 0]
    grad_key_rows = grad_qkv[:, 1]
    grad_value_rows = grad_qkv[:, 2]
    grad_resid = grad_first_in + jnp.einsum(
        "te,de->td", grad_query_rows, back_query, preferred_element_type=jnp.float32
    )
    grad_resid = grad_resid + jnp.einsum(
        "te,de->td", grad_key_rows, back_key, preferred_element_type=jnp.float32
    )
    grad_resid = grad_resid + jnp.einsum(
        "te,de->td", grad_value_rows, back_value, preferred_element_type=jnp.float32
    )
    grad_tokens = grad_resid.astype(jnp.bfloat16)
    grad_time = jnp.sum(grad_resid.reshape(item_count, slot_count, model_width), axis=1).astype(
        jnp.bfloat16
    )
    term_in = jnp.einsum("tf,td->fd", grad_pre, first_low, preferred_element_type=jnp.float32)
    term_down = jnp.einsum("tf,td->fd", hidden_low, grad_ffn, preferred_element_type=jnp.float32)
    ffn_share = lax.psum_scatter(
        jnp.concatenate([term_in, term_down], axis=1).astype(jnp.bfloat16),
        "seq",
        scatter_dimension=0,
        tiled=True,
    ).astype(jnp.float32)
    share_in = ffn_share[:, :model_width]
    share_down = ffn_share[:, model_width:]
    grad_qkv_flat = grad_qkv.reshape(token_count, 3 * model_width)
    term_qkv = jnp.einsum("tr,te->re", resid_low, grad_qkv_flat, preferred_element_type=jnp.float32)
    term_out = jnp.einsum("tr,te->re", mixed_rows, grad_attn, preferred_element_type=jnp.float32)
    term_time = jnp.einsum("tr,te->re", time_embed, grad_time, preferred_element_type=jnp.float32)
    attn_share = lax.psum_scatter(
        jnp.concatenate([term_qkv, term_out, term_time], axis=1).astype(jnp.bfloat16),
        "seq",
        scatter_dimension=0,
        tiled=True,
    ).astype(jnp.float32)
    sum_in, sum_down, sum_attn = lax.psum((share_in, share_down, attn_share), "dp")
    (
        grad_b_query,
        grad_b_value,
        grad_b_out,
        grad_b_time,
        grad_b_in,
        grad_b_down,
        sum_gain_one,
        sum_shift_one,
        sum_gain_two,
        sum_shift_two,
    ) = lax.psum(
        (
            jnp.sum(grad_query_rows, axis=0, dtype=jnp.float32),
            jnp.sum(grad_value_rows, axis=0, dtype=jnp.float32),
            jnp.sum(grad_attn, axis=0, dtype=jnp.float32),
            jnp.sum(grad_time, axis=0, dtype=jnp.float32),
            jnp.sum(grad_pre, axis=0, dtype=jnp.float32),
            jnp.sum(grad_ffn, axis=0, dtype=jnp.float32),
            grad_gain_one,
            grad_shift_one,
            grad_gain_two,
            grad_shift_two,
        ),
        ("dp", "seq"),
    )
    return (
        layer_out,
        grad_tokens,
        sum_attn[:, :model_width],
        sum_attn[:, model_width : 2 * model_width],
        sum_attn[:, 2 * model_width : 3 * model_width],
        sum_attn[:, 3 * model_width : 4 * model_width],
        sum_attn[:, 4 * model_width :],
        sum_in,
        sum_down,
        grad_b_query,
        grad_b_value,
        grad_b_out,
        grad_b_time,
        grad_b_in,
        grad_b_down,
        sum_gain_one,
        sum_shift_one,
        sum_gain_two,
        sum_shift_two,
    )


def solution(mesh):
    in_specs = (
        P(("dp", "seq"), None),
        P(("dp", "seq"), None),
        P("dp"),
        P(("dp", "seq"), None),
        P("seq", None),
        P("seq", None),
        P("seq", None),
        P("seq", None),
        P("seq", None),
        P("seq", None),
        P("seq", None),
        P(),
        P(),
        P(),
        P(),
        P(),
        P(),
        P(),
        P(),
        P(),
        P(),
    )
    out_specs = (
        P(("dp", "seq"), None),
        P(("dp", "seq"), None),
        P("seq", None),
        P("seq", None),
        P("seq", None),
        P("seq", None),
        P("seq", None),
        P("seq", None),
        P("seq", None),
        P(),
        P(),
        P(),
        P(),
        P(),
        P(),
        P(),
        P(),
        P(),
        P(),
    )
    return jax.shard_map(local, mesh=mesh, in_specs=in_specs, out_specs=out_specs, check_vma=False)
```

profile of v0, /device:TPU:0, one launch (start us, length us, event | category | flops | bytes accessed | tf_op | source)
XLA Modules:
  0.0 1024.9 jit_solution(11175937221474394372)
XLA Ops:
  11.2 23.7 %all-gather.8.cloned.1.call-done = bf16[1024,1024]{1,0:T(8,128)(2,1)} async-done(((bf16[256,1024]{1,0:T(8,128)(2,1)}), bf16[1024,1024]{1,0:T(8,128)(2,1)}) %all-gather.8.cloned.1.call-update) | async-done | bytes 2097168 | tf_op jit(solution)/shard_map/all_gather | solution.py:122
  36.9 22.2 %all-gather.12.cloned.1.call-done = bf16[1024,1024]{1,0:T(8,128)(2,1)} async-done(((bf16[256,1024]{1,0:T(8,128)(2,1)}), bf16[1024,1024]{1,0:T(8,128)(2,1)}) %all-gather.12.cloned.1.call-update) | async-done | bytes 2097168 | tf_op jit(solution)/shard_map/all_gather | solution.py:119
  62.9 20.3 %all-gather.10.cloned.1.call-done = bf16[1024,1024]{1,0:T(8,128)(2,1)} async-done(((bf16[256,1024]{1,0:T(8,128)(2,1)}), bf16[1024,1024]{1,0:T(8,128)(2,1)}) %all-gather.10.cloned.1.call-update) | async-done | bytes 2097168 | tf_op jit(solution)/shard_map/all_gather | solution.py:118
  87.1 20.2 %all-gather.14.cloned.1.call-done = bf16[1024,1024]{1,0:T(8,128)(2,1)} async-done(((bf16[256,1024]{1,0:T(8,128)(2,1)}), bf16[1024,1024]{1,0:T(8,128)(2,1)}) %all-gather.14.cloned.1.call-update) | async-done | bytes 2097168 | tf_op jit(solution)/shard_map/all_gather | solution.py:120
  122.3 77.5 %all-to-all-done = bf16[1,512,3,1024]{1,2,0,3:T(4,128)(2,1)} async-done(((bf16[1,512,3,1024]{1,2,0,3:T(4,128)(2,1)}), bf16[1,512,3,1024]{1,2,0,3:T(4,128)(2,1)}, u32[]{:S(2)}, u32[]{:S(2)}) %all-to-all-start) | async-done | bytes 3145760 | tf_op jit(solution)/shard_map/all_to_all | solution.py:155
  202.9 16.3 %while.22 = (s32[]{:T(128)}, bf16[4,512,256]{1,2,0:T(8,128)(2,1)}, f32[4,4,512]{2,1,0:T(4,128)S(1)}, bf16[4,512,3,256]{1,3,2,0:T(8,128)(2,1)S(1)}, pred[4,512]{1,0:T(4,128)(4,1)S(1)}, /*index=5*/s32[]{:T(128)}) while((s32[]{:T(128)}, bf16[4,512,256]{1,2,0:T(8,128)(2,1)}, f32[4,4,512]{2,1,0:T(4,128)S(1)}, ...), condition=%wide.region_3.4_spmd, body=%wide.region_0.3_spmd.sunk | while | flops 281147392 | bytes 17370192 | solution.py:156
  223.7 18.0 %all-to-all-done.1 = bf16[4,512,256]{1,2,0:T(8,128)(2,1)} async-done(((bf16[4,512,256]{1,2,0:T(8,128)(2,1)}), bf16[4,512,256]{1,2,0:T(8,128)(2,1)}, u32[]{:S(2)}, u32[]{:S(2)}) %all-to-all-start.1) | async-done | bytes 1048608 | tf_op jit(solution)/shard_map/all_to_all | solution.py:157
  247.0 27.2 %multiply_convert_fusion.1 = (bf16[512,4096]{1,0:T(8,128)(2,1)}, f32[512,4096]{1,0:T(8,128)}, f32[512,4096]{1,0:T(8,128)}) fusion(f32[4096]{0:T(1024)S(1)} %convert_element_type.170, bf16[4096,1024]{1,0:T(8,128)(2,1)} %all-gather.18.cloned.1.call-done, f32[512,1024]{1,0:T(8,128)} %copy-done, f32[1024]{0:T(1024)S(1)} %convert_element_type.168, ...), kind=kOutput, calls=%fused_computation.37 | convolution fusion | flops 4436000768 | bytes 31485952 | tf_op jit(solution)/shard_map/td,fd->tf/dot_general | solution.py:164
  274.2 10.3 %all-gather.20.cloned.1.call-done = bf16[4096,1024]{1,0:T(8,128)(2,1)} async-done(((bf16[1024,1024]{1,0:T(8,128)(2,1)}), bf16[4096,1024]{1,0:T(8,128)(2,1)}) %all-gather.20.cloned.1.call-update) | async-done | bytes 8388624 | tf_op jit(solution)/shard_map/all_gather | solution.py:124
  284.5 10.0 fusion.59
  300.6 7.1 convolution_convert_fusion
  307.7 13.5 %convert_reduce_fusion = (f32[4096]{0:T(1024)S(1)}, bf16[512,4096]{1,0:T(8,128)(2,1)S(1)}) fusion(f32[512,4096]{1,0:T(8,128)} %get-tuple-element.209, f32[512,4096]{1,0:T(8,128)} %get-tuple-element.234, f32[4096]{0:T(1024)S(1)} %convert_element_type.170, bf16[512,1024]{1,0:T(8,128)(2,1)S(1)} %get-tuple-element.199, ...), kind=kOutput, calls=%fused_computation.35 | convolution fusion | flops 4330614784 | bytes 30441472 | tf_op jit(solution)/shard_map/td,fd->tf/dot_general | solution.py:183
  321.3 7.0 convolution_convert_fusion.1
  328.3 13.9 %pad_maximum_fusion = bf16[4096,2048]{0,1:T(8,128)(2,1)} fusion(bf16[4096,1024]{0,1:T(8,128)(2,1)} %convolution_convert_fusion, bf16[4096,1024]{0,1:T(8,128)(2,1)} %convolution_convert_fusion.1), kind=kLoop, calls=%fused_computation.31 | loop fusion | flops 33554432 | bytes 33554432 | tf_op jit(solution)/shard_map/concatenate | solution.py:221
  342.2 11.4 %multiply_reduce_fusion.2 = (f32[1024]{0:T(1024)S(1)}, f32[512]{0:T(512)S(1)}, f32[1024]{0:T(1024)S(1)}, f32[512,1024]{1,0:T(8,128)S(1)}) fusion(f32[512,1024]{1,0:T(8,128)} %copy-done, f32[512]{0:T(512)S(1)} %fusion.42, f32[512]{0:T(512)S(1)} %broadcast_multiply_fusion.1, f32[1024]{0:T(1024)S(1)} %convert_element_type.167, ...), kind=kOutput, calls=%fused_computation.61 | convolution fusion | flops 4300207616 | bytes 18894848 | tf_op jit(solution)/shard_map/dot_general | solution.py:185
  365.9 9.0 reduce.7
  383.1 26.1 %all-to-all-done.2 = bf16[4,2,65536]{2,1,0:T(2,128)(2,1)} async-done(((bf16[4,2,65536]{2,1,0:T(2,128)(2,1)}), bf16[4,2,65536]{2,1,0:T(2,128)(2,1)}, u32[]{:S(2)}, u32[]{:S(2)}) %all-to-all-start.2) | async-done | bytes 1048608 | tf_op jit(solution)/shard_map/all_to_all | solution.py:191
  416.1 35.0 %while.23 = (s32[]{:T(128)}, bf16[4,512,3,256]{1,3,2,0:T(8,128)(2,1)}, bf16[4,512,3,256]{1,3,2,0:T(8,128)(2,1)S(1)}, pred[4,512]{1,0:T(4,128)(4,1)S(1)}, f32[4,4...) while((s32[]{:T(128)}, bf16[4,512,3,256]{1,3,2,0:T(8,128)(2,1)}, ...), condition=%wide.region_14.15_spmd, body=%wide.region_12.14_spmd.sunk | while | flops 689829888 | bytes 39382108 | solution.py:198
  459.2 51.5 %all-to-all-done.3 = bf16[4,512,3,256]{1,3,2,0:T(8,128)(2,1)S(1)} async-done(((bf16[4,512,3,256]{1,3,2,0:T(8,128)(2,1)}), bf16[4,512,3,256]{1,3,2,0:T(8,128)(2,1)S(1)}, u32[]{:S(2)}, u32[]{:S(2)}) %all-to-all-start.3) | async-done | bytes 3145760 | tf_op jit(solution)/shard_map/all_to_all | solution.py:199
  524.0 9.9 pad_maximum_fusion.1
  548.6 41.3 %all-reduce = (f32[1024]{0:T(1024)}, f32[1024]{0:T(1024)}, f32[1024]{0:T(1024)}, f32[1024]{0:T(1024)}, f32[4096]{0:T(1024)}, /*index=5*/f32[1024]{0:T(1024)}, f3...) all-reduce(f32[1024]{0:T(1024)S(1)} %get-tuple-element.240, ...), channel_id=1, replica_groups=mesh['dp'=8,'seq'=4] {'dp','seq'}, use_global_device_ids=true, to_apply=%region_22.23 | all-reduce | flops 13312 | bytes 104448 | tf_op jit(solution)/shard_map/psum | solution.py:250
  589.9 29.4 %reduce-scatter.3.cloned.1.call-done = bf16[256,5120]{1,0:T(8,128)(2,1)} async-done(((bf16[1024,5120]{1,0:T(8,128)(2,1)}), bf16[256,5120]{1,0:T(8,128)(2,1)}) %reduce-scatter.3.cloned.1.call-update) | async-done | bytes 2621456 | tf_op jit(solution)/shard_map/reduce_scatter | solution.py:232
  619.3 267.7 %all-reduce.6 = f32[256,5120]{1,0:T(8,128)} all-reduce(bf16[256,5120]{1,0:T(8,128)(2,1)} %reduce-scatter.3.cloned.1.call-done), channel_id=1, replica_groups=mesh['dp'=8,'seq'=4] {'dp'}, use_global_device_ids=true, to_apply=%region_17.18 | all-reduce | flops 1310720 | bytes 7864320 | tf_op jit(solution)/shard_map/psum | solution.py:238
  892.0 114.9 %all-reduce.5.cloned.1.call-done = (f32[1024,1024]{0,1:T(8,128)}, f32[1024,1024]{0,1:T(8,128)}) async-done(((f32[1024,1024]{0,1:T(8,128)}, f32[1024,1024]{0,1:T(8,128)}), (f32[1024,1024]{0,1:T(8,128)}, f32[1024,1024]{0,1:T(8,128)})) %all-reduce.5.cloned.1.call-update) | async-done | bytes 8388624 | tf_op jit(solution)/shard_map/psum | solution.py:238
  (250 shorter events, 177.1 us)
Async XLA Ops:
  7.2 27.7 %copy-start.22 = (bf16[1,1024]{1,0:T(2,128)(2,1)S(1)}, bf16[1,1024]{1,0:T(2,128)(2,1)}, u32[]{:S(2)}) copy-start(bf16[1,1024]{1,0:T(2,128)(2,1)} %param.26) | copy-start | bytes 6148
  7.2 29.7 %copy-start.27 = (bf16[1024]{0:T(1024)(128)(2,1)S(1)}, bf16[1024]{0:T(1024)(128)(2,1)}, u32[]{:S(2)}) copy-start(bf16[1024]{0:T(1024)(128)(2,1)} %param.39) | copy-start | bytes 6148
  7.2 51.9 %copy-start.12 = (bf16[512,1024]{1,0:T(8,128)(2,1)S(1)}, bf16[512,1024]{1,0:T(8,128)(2,1)}, u32[]{:S(2)}) copy-start(bf16[512,1024]{1,0:T(8,128)(2,1)} %param.25) | copy-start | bytes 3145732
  7.2 27.7 %all-gather.8.cloned.1.call-start = ((), (), s32[]{:S(2)}) async-start(), calls=%async_computation.6 | async-start | bytes 2621440 | tf_op jit(solution)/shard_map/all_gather | solution.py:122
  8.0 51.1 %all-gather.12.cloned.1.call-start = ((), (), s32[]{:S(2)}) async-start(), calls=%async_computation.8 | async-start | bytes 2621440 | tf_op jit(solution)/shard_map/all_gather | solution.py:119
  8.7 74.5 %all-gather.10.cloned.1.call-start = ((), (), s32[]{:S(2)}) async-start(), calls=%async_computation.7 | async-start | bytes 2621440 | tf_op jit(solution)/shard_map/all_gather | solution.py:118
  9.5 97.8 %all-gather.14.cloned.1.call-start = ((), (), s32[]{:S(2)}) async-start(), calls=%async_computation.9 | async-start | bytes 2621440 | tf_op jit(solution)/shard_map/all_gather | solution.py:120
  10.0 213.6 %all-gather.16.cloned.1.call-start = ((), (), s32[]{:S(2)}) async-start(), calls=%async_computation.10 | async-start | bytes 2621440 | tf_op jit(solution)/shard_map/all_gather | solution.py:121
  10.6 236.4 %all-gather.18.cloned.1.call-start = ((), (), s32[]{:S(2)}) async-start(), calls=%async_computation.11 | async-start | bytes 10485760 | tf_op jit(solution)/shard_map/all_gather | solution.py:123
  36.9 204.8 %copy-start.16 = (f32[1024]{0:T(1024)}, f32[1024]{0:T(1024)S(1)}, u32[]{:S(2)}) copy-start(f32[1024]{0:T(1024)S(1)} %convert_add_fusion.1) | copy-start | bytes 12292
  116.3 83.5 %all-to-all-start = ((bf16[1,512,3,1024]{1,2,0,3:T(4,128)(2,1)}), bf16[1,512,3,1024]{1,2,0,3:T(4,128)(2,1)}, u32[]{:S(2)}, u32[]{:S(2)}) async-start(bf16[1,512,3,1024]{1,2,0,3:T(4,128)(2,1)} %copy.80), calls=%async_computation | async-start | bytes 8388608 | tf_op jit(solution)/shard_map/all_to_all | solution.py:155
  121.4 163.1 %all-gather.20.cloned.1.call-start = ((), (), s32[]{:S(2)}) async-start(), calls=%async_computation.12 | async-start | bytes 10485760 | tf_op jit(solution)/shard_map/all_gather | solution.py:124
  202.8 20.7 %copy-start.29 = (bf16[1024]{0:T(1024)(128)(2,1)S(1)}, bf16[1024]{0:T(1024)(128)(2,1)}, u32[]{:S(2)}) copy-start(bf16[1024]{0:T(1024)(128)(2,1)} %param.42) | copy-start | bytes 6148
  202.8 20.7 %copy-start.30 = (bf16[1024]{0:T(1024)(128)(2,1)S(1)}, bf16[1024]{0:T(1024)(128)(2,1)}, u32[]{:S(2)}) copy-start(bf16[1024]{0:T(1024)(128)(2,1)} %param.43) | copy-start | bytes 6148
  202.8 20.7 %copy-start.24 = (bf16[4096]{0:T(1024)(128)(2,1)S(1)}, bf16[4096]{0:T(1024)(128)(2,1)}, u32[]{:S(2)}) copy-start(bf16[4096]{0:T(1024)(128)(2,1)} %param.40) | copy-start | bytes 24580
  202.8 20.7 %copy-start.31 = (bf16[1024]{0:T(1024)(128)(2,1)S(1)}, bf16[1024]{0:T(1024)(128)(2,1)}, u32[]{:S(2)}) copy-start(bf16[1024]{0:T(1024)(128)(2,1)} %param.41) | copy-start | bytes 6148
  202.9 20.7 %copy-start.32 = (bf16[1024]{0:T(1024)(128)(2,1)S(1)}, bf16[1024]{0:T(1024)(128)(2,1)}, u32[]{:S(2)}) copy-start(bf16[1024]{0:T(1024)(128)(2,1)} %param.44) | copy-start | bytes 6148
  202.9 20.7 %copy-start.33 = (bf16[1024]{0:T(1024)(128)(2,1)S(1)}, bf16[1024]{0:T(1024)(128)(2,1)}, u32[]{:S(2)}) copy-start(bf16[1024]{0:T(1024)(128)(2,1)} %param.45) | copy-start | bytes 6148
  219.2 22.5 %all-to-all-start.1 = ((bf16[4,512,256]{1,2,0:T(8,128)(2,1)}), bf16[4,512,256]{1,2,0:T(8,128)(2,1)}, u32[]{:S(2)}, u32[]{:S(2)}) async-start(bf16[4,512,256]{1,2,0:T(8,128)(2,1)} %get-tuple-element.79), calls=%async_computation.1 | async-start | bytes 2097152 | tf_op jit(solution)/shard_map/all_to_all | solution.py:157
  223.4 310.5 %reduce-scatter.5.cloned.1.call-start = ((), (), s32[]{:S(2)}) async-start(), calls=%async_computation.14 | async-start | bytes 20971520 | tf_op jit(solution)/shard_map/reduce_scatter | solution.py:220
  378.8 30.4 %all-to-all-start.2 = ((bf16[4,2,65536]{2,1,0:T(2,128)(2,1)}), bf16[4,2,65536]{2,1,0:T(2,128)(2,1)}, u32[]{:S(2)}, u32[]{:S(2)}) async-start(bf16[4,2,65536]{2,1,0:T(2,128)(2,1)} %reshape.269), calls=%async_computation.2 | async-start | bytes 2097152 | tf_op jit(solution)/shard_map/all_to_all | solution.py:191
  451.1 59.6 %all-to-all-start.3 = ((bf16[4,512,3,256]{1,3,2,0:T(8,128)(2,1)}), bf16[4,512,3,256]{1,3,2,0:T(8,128)(2,1)S(1)}, u32[]{:S(2)}, u32[]{:S(2)}) async-start(bf16[4,512,3,256]{1,3,2,0:T(8,128)(2,1)} %get-tuple-element.81), calls=%async_computation.3 | async-start | bytes 6291456 | tf_op jit(solution)/shard_map/all_to_all | solution.py:199
  454.9 164.4 %reduce-scatter.3.cloned.1.call-start = ((), (), s32[]{:S(2)}) async-start(), calls=%async_computation.13 | async-start | bytes 13107200 | tf_op jit(solution)/shard_map/reduce_scatter | solution.py:232
  533.9 473.0 %all-reduce.5.cloned.1.call-start = ((), (), s32[]{:S(2)}) async-start(), calls=%async_computation.15 | async-start | bytes 16777216 | tf_op jit(solution)/shard_map/psum | solution.py:238
  (30 other events, 144.6 us)
Sparse Core Ops, SparseCore 0:
  9.6 25.2 all-gather.7
  36.5 22.5 all-gather.11
  60.7 22.5 all-gather.9
  84.7 22.5 all-gather.13
  108.7 27.7 all-gather.15
  137.9 83.4 all-gather.17
  223.0 61.5 all-gather.19
  342.3 155.0 reduce-scatter.4
  534.0 85.2 reduce-scatter.2
  624.4 382.4 all-reduce.4
where the time goes:
time: 1030 us; the launch traced here: 1020 us
  waiting for transfers between devices  419 us (41%)
  blocking collectives  309 us (30%)
  matrix products  135 us (13%)
  local copies, waits for them, and re-layouts  75.6 us (7%)
  other arithmetic  52.9 us (5%)
  starting transfers between devices  17.8 us (2%)
  between operations  15.3 us (1%)
    psum x1, blocking collectives, local(): lax.psum((share_in, share_down, attn_share), 'dp')  268 us
    psum x1, waiting for transfers between devices, local(): lax.psum((share_in, share_down, attn_share), 'dp')  115 us
    all_to_all x1, waiting for transfers between devices, local(): lax.all_to_all(stacked, 'seq', split_axis=3, concat_axis=0, tiled=True)  77.5 us
    all_to_all x1, waiting for transfers between devices, local(): lax.all_to_all(grad_stack, 'seq', split_axis=0, concat_axis=3, tiled=True)  51.5 us
    psum x1, blocking collectives, local(): lax.psum((jnp.sum(grad_query_rows, axis=0, dtype=jnp.float32), jnp.sum(gr...  41.3 us
    unnamed x86, local copies, waits for them, and re-layouts  32.8 us
    reduce_scatter x1, waiting for transfers between devices, local(): lax.psum_scatter(jnp.concatenate([term_qkv, term_out, term_time], axis=1)...  29.4 us
    dot_general x1, matrix products, local(): jnp.einsum('td,fd->tf', first_low, full_in, preferred_element_type=jnp.fl...  27.2 us
  transfers between devices with their start and end apart: 14, of which 11 were waited for; matrix products, arithmetic and copies ran while one was open for 18% of the time, Pallas kernels for 0%

commit v1 on v0

--- a/solution.py
+++ b/solution.py
@@ -7,6 +7,14 @@
 BLOCK = 25
 norm_eps = 1e-05
 neg_large = -1e30
+
+
+def view_things(state, in_dim):
+    state = jnp.moveaxis(state, 0, in_dim)
+    step_out = state.shape
+    return state.reshape(
+        *step_out[:in_dim], step_out[in_dim] * step_out[in_dim + 1], *step_out[in_dim + 2 :]
+    )
 
 
 def layer_norm(values, gain, shift):
@@ -109,6 +117,26 @@
     gain_two,
     shift_two,
 ):
+
+    def put_scales_now(a0, peer_axis, dim_k):
+        fan = lax.axis_size(peer_axis)
+        so_far_all = [(it, (it + 1) % fan) for it in range(fan)]
+        log = [(j0, c) for c, j0 in so_far_all]
+        state_next, long_array = ([], [])
+        for nth in [*range(fan - 1)]:
+            if nth % 2 == 0:
+                state_next.append(
+                    lax.ppermute(state_next[-1] if state_next else a0, peer_axis, perm=so_far_all)
+                )
+            else:
+                long_array.append(
+                    lax.ppermute(long_array[-1] if long_array else a0, peer_axis, log)
+                )
+        lower = jnp.stack([*state_next[::-1], a0, *long_array])
+        carry_in = lax.axis_index(peer_axis) - len(state_next)
+        lower = lower[(jnp.arange(fan) - carry_in) % fan]
+        return view_things(lower, dim_k)
+
     seq_rank = lax.axis_index("seq")
     item_count = time_embed.shape[0]
     token_count = tokens.shape[0]
@@ -119,7 +147,7 @@
         lax.all_gather(w_key, "seq", axis=0, tiled=True),
         lax.all_gather(w_value, "seq", axis=0, tiled=True),
         lax.all_gather(w_out, "seq", axis=0, tiled=True),
-        lax.all_gather(w_time, "seq", axis=0, tiled=True),
+        put_scales_now(w_time, "seq", 0),
         lax.all_gather(w_in, "seq", axis=0, tiled=True),
         lax.all_gather(w_down, "seq", axis=0, tiled=True),
     )

time: 1030 us -> 1020 us (level)
  waiting for transfers between devices: 419 us -> 389 us
    all_gather x1 -> x0, waiting for transfers between devices: 23.7 us -> none  [local(): lax.all_gather(w_time, 'seq', axis=0, tiled=True)]
    ppermute x0 -> x3, waiting for transfers between devices: none -> 22.2 us  [the longest x2 22.2 us: put_scales_now(): lax.ppermute(state_next[-1] if state_next else a0, peer_axis, perm=so_far...]
    all_gather x1, waiting for transfers between devices: 22.2 us -> 0.02 us  [local(): lax.all_gather(w_key, 'seq', axis=0, tiled=True)]
    unnamed x86 -> x92, local copies, waits for them, and re-layouts: 32.8 us -> 34.2 us
  transfers between devices with their start and end apart: 14 -> 16, of which waited for: 11 -> 12; matrix products, arithmetic and copies ran while one was open for 18% -> 19% of each run, Pallas kernels for 0% -> 0%
where the time goes in v1:
time: 1020 us; the launch traced here: 1010 us
  waiting for transfers between devices  389 us (38%)
  blocking collectives  308 us (30%)
  matrix products  135 us (13%)
  local copies, waits for them, and re-layouts  79 us (8%)
  other arithmetic  54.4 us (5%)
  starting transfers between devices  27.3 us (3%)
  between operations  15 us (1%)
    psum x1, blocking collectives, local(): lax.psum((share_in, share_down, attn_share), 'dp')  266 us
    psum x1, waiting for transfers between devices, local(): lax.psum((share_in, share_down, attn_share), 'dp')  116 us
    all_to_all x1, waiting for transfers between devices, local(): lax.all_to_all(stacked, 'seq', split_axis=3, concat_axis=0, tiled=True)  77.7 us
    all_to_all x1, waiting for transfers between devices, local(): lax.all_to_all(grad_stack, 'seq', split_axis=0, concat_axis=3, tiled=True)  50.7 us
    psum x1, blocking collectives, local(): lax.psum((jnp.sum(grad_query_rows, axis=0, dtype=jnp.float32), jnp.sum(gr...  41.3 us
    unnamed x92, local copies, waits for them, and re-layouts  34.2 us
    reduce_scatter x1, waiting for transfers between devices, local(): lax.psum_scatter(jnp.concatenate([term_qkv, term_out, term_time], axis=1)...  29.4 us
    dot_general x1, matrix products, local(): jnp.einsum('td,fd->tf', first_low, full_in, preferred_element_type=jnp.fl...  27.2 us
  transfers between devices with their start and end apart: 16, of which 12 were waited for; matrix products, arithmetic and copies ran while one was open for 19% of the time, Pallas kernels for 0%

profile of v1, /device:TPU:0, one launch (start us, length us, event | category | flops | bytes accessed | tf_op | source)
XLA Modules:
  0.0 1008.2 jit_solution(9404630528829147486)
XLA Ops:
  13.2 10.6 %collective-permute-done = bf16[256,1024]{1,0:T(8,128)(2,1)S(1)} collective-permute-done((bf16[256,1024]{1,0:T(8,128)(2,1)S(1)}, bf16[256,1024]{1,0:T(8,128)(2,1)S(1)}, u32[]{:S(2)}, u32[]{:S(2)}) %collective-permute-start) | collective-permute-done | bytes 524320 | tf_op jit(solution)/shard_map/ppermute | solution.py:129
  30.9 11.6 %collective-permute-done.1 = bf16[256,1024]{1,0:T(8,128)(2,1)S(1)} collective-permute-done((bf16[256,1024]{1,0:T(8,128)(2,1)S(1)}, bf16[256,1024]{1,0:T(8,128)(2,1)S(1)}, u32[]{:S(2)}, u32[]{:S(2)}) %collective-permute-start.1) | collective-permute-done | bytes 524320 | tf_op jit(solution)/shard_map/ppermute | solution.py:129
  52.6 14.3 %all-gather.7.cloned.1.call-done = bf16[1024,1024]{1,0:T(8,128)(2,1)} async-done(((bf16[256,1024]{1,0:T(8,128)(2,1)}), bf16[1024,1024]{1,0:T(8,128)(2,1)}) %all-gather.7.cloned.1.call-update) | async-done | bytes 2097168 | tf_op jit(solution)/shard_map/all_gather | solution.py:146
  70.7 20.3 %all-gather.11.cloned.1.call-done = bf16[1024,1024]{1,0:T(8,128)(2,1)} async-done(((bf16[256,1024]{1,0:T(8,128)(2,1)}), bf16[1024,1024]{1,0:T(8,128)(2,1)}) %all-gather.11.cloned.1.call-update) | async-done | bytes 2097168 | tf_op jit(solution)/shard_map/all_gather | solution.py:148
  105.9 77.7 %all-to-all-done = bf16[1,512,3,1024]{1,2,0,3:T(4,128)(2,1)} async-done(((bf16[1,512,3,1024]{1,2,0,3:T(4,128)(2,1)}), bf16[1,512,3,1024]{1,2,0,3:T(4,128)(2,1)}, u32[]{:S(2)}, u32[]{:S(2)}) %all-to-all-start) | async-done | bytes 3145760 | tf_op jit(solution)/shard_map/all_to_all | solution.py:183
  186.7 16.3 %while.22 = (s32[]{:T(128)}, bf16[4,512,256]{1,2,0:T(8,128)(2,1)}, f32[4,4,512]{2,1,0:T(4,128)S(1)}, bf16[4,512,3,256]{1,3,2,0:T(8,128)(2,1)S(1)}, pred[4,512]{1,0:T(4,128)(4,1)S(1)}, /*index=5*/s32[]{:T(128)}) while((s32[]{:T(128)}, bf16[4,512,256]{1,2,0:T(8,128)(2,1)}, f32[4,4,512]{2,1,0:T(4,128)S(1)}, ...), condition=%wide.region_3.4_spmd, body=%wide.region_0.3_spmd.sunk | while | flops 281147392 | bytes 17370192 | solution.py:184
  207.5 18.2 %all-to-all-done.1 = bf16[4,512,256]{1,2,0:T(8,128)(2,1)} async-done(((bf16[4,512,256]{1,2,0:T(8,128)(2,1)}), bf16[4,512,256]{1,2,0:T(8,128)(2,1)}, u32[]{:S(2)}, u32[]{:S(2)}) %all-to-all-start.1) | async-done | bytes 1048608 | tf_op jit(solution)/shard_map/all_to_all | solution.py:185
  231.0 27.2 %multiply_convert_fusion.1 = (bf16[512,4096]{1,0:T(8,128)(2,1)}, f32[512,4096]{1,0:T(8,128)}, f32[512,4096]{1,0:T(8,128)}) fusion(f32[4096]{0:T(1024)S(1)} %convert_element_type.170, bf16[4096,1024]{1,0:T(8,128)(2,1)} %all-gather.15.cloned.1.call-done, f32[512,1024]{1,0:T(8,128)} %copy-done, f32[1024]{0:T(1024)S(1)} %convert_element_type.168, ...), kind=kOutput, calls=%fused_computation.38 | convolution fusion | flops 4436000768 | bytes 31485952 | tf_op jit(solution)/shard_map/td,fd->tf/dot_general | solution.py:192
  258.2 10.2 %all-gather.17.cloned.1.call-done = bf16[4096,1024]{1,0:T(8,128)(2,1)} async-done(((bf16[1024,1024]{1,0:T(8,128)(2,1)}), bf16[4096,1024]{1,0:T(8,128)(2,1)}) %all-gather.17.cloned.1.call-update) | async-done | bytes 8388624 | tf_op jit(solution)/shard_map/all_gather | solution.py:152
  268.4 10.0 fusion.61
  284.4 7.2 convolution_convert_fusion
  291.6 13.5 %convert_reduce_fusion = (f32[4096]{0:T(1024)S(1)}, bf16[512,4096]{1,0:T(8,128)(2,1)S(1)}) fusion(f32[512,4096]{1,0:T(8,128)} %get-tuple-element.209, f32[512,4096]{1,0:T(8,128)} %get-tuple-element.234, f32[4096]{0:T(1024)S(1)} %convert_element_type.170, bf16[512,1024]{1,0:T(8,128)(2,1)S(1)} %get-tuple-element.199, ...), kind=kOutput, calls=%fused_computation.36 | convolution fusion | flops 4330614784 | bytes 30441472 | tf_op jit(solution)/shard_map/td,fd->tf/dot_general | solution.py:211
  305.1 7.0 convolution_convert_fusion.1
  312.1 13.8 %pad_maximum_fusion = bf16[4096,2048]{0,1:T(8,128)(2,1)} fusion(bf16[4096,1024]{0,1:T(8,128)(2,1)} %convolution_convert_fusion, bf16[4096,1024]{0,1:T(8,128)(2,1)} %convolution_convert_fusion.1), kind=kLoop, calls=%fused_computation.32 | loop fusion | flops 33554432 | bytes 33554432 | tf_op jit(solution)/shard_map/concatenate | solution.py:249
  326.0 11.4 %multiply_reduce_fusion.2 = (f32[1024]{0:T(1024)S(1)}, f32[512]{0:T(512)S(1)}, f32[1024]{0:T(1024)S(1)}, f32[512,1024]{1,0:T(8,128)S(1)}) fusion(f32[512,1024]{1,0:T(8,128)} %copy-done, f32[512]{0:T(512)S(1)} %fusion.42, f32[512]{0:T(512)S(1)} %broadcast_multiply_fusion.1, f32[1024]{0:T(1024)S(1)} %convert_element_type.167, ...), kind=kOutput, calls=%fused_computation.63 | convolution fusion | flops 4300207616 | bytes 18894848 | tf_op jit(solution)/shard_map/dot_general | solution.py:213
  350.3 9.0 reduce.7
  367.5 26.1 %all-to-all-done.2 = bf16[4,2,65536]{2,1,0:T(2,128)(2,1)} async-done(((bf16[4,2,65536]{2,1,0:T(2,128)(2,1)}), bf16[4,2,65536]{2,1,0:T(2,128)(2,1)}, u32[]{:S(2)}, u32[]{:S(2)}) %all-to-all-start.2) | async-done | bytes 1048608 | tf_op jit(solution)/shard_map/all_to_all | solution.py:219
  400.4 35.0 %while.23 = (s32[]{:T(128)}, bf16[4,512,3,256]{1,3,2,0:T(8,128)(2,1)}, bf16[4,512,3,256]{1,3,2,0:T(8,128)(2,1)S(1)}, pred[4,512]{1,0:T(4,128)(4,1)S(1)}, f32[4,4...) while((s32[]{:T(128)}, bf16[4,512,3,256]{1,3,2,0:T(8,128)(2,1)}, ...), condition=%wide.region_14.15_spmd, body=%wide.region_12.14_spmd.sunk | while | flops 689829888 | bytes 39382108 | solution.py:226
  443.7 50.7 %all-to-all-done.3 = bf16[4,512,3,256]{1,3,2,0:T(8,128)(2,1)S(1)} async-done(((bf16[4,512,3,256]{1,3,2,0:T(8,128)(2,1)}), bf16[4,512,3,256]{1,3,2,0:T(8,128)(2,1)S(1)}, u32[]{:S(2)}, u32[]{:S(2)}) %all-to-all-start.3) | async-done | bytes 3145760 | tf_op jit(solution)/shard_map/all_to_all | solution.py:227
  507.8 9.9 pad_maximum_fusion.1
  532.4 41.3 %all-reduce = (f32[1024]{0:T(1024)}, f32[1024]{0:T(1024)}, f32[1024]{0:T(1024)}, f32[1024]{0:T(1024)}, f32[4096]{0:T(1024)}, /*index=5*/f32[1024]{0:T(1024)}, f3...) all-reduce(f32[1024]{0:T(1024)S(1)} %get-tuple-element.240, ...), channel_id=1, replica_groups=mesh['dp'=8,'seq'=4] {'dp','seq'}, use_global_device_ids=true, to_apply=%region_22.23 | all-reduce | flops 13312 | bytes 104448 | tf_op jit(solution)/shard_map/psum | solution.py:278
  573.7 29.4 %reduce-scatter.3.cloned.1.call-done = bf16[256,5120]{1,0:T(8,128)(2,1)} async-done(((bf16[1024,5120]{1,0:T(8,128)(2,1)}), bf16[256,5120]{1,0:T(8,128)(2,1)}) %reduce-scatter.3.cloned.1.call-update) | async-done | bytes 2621456 | tf_op jit(solution)/shard_map/reduce_scatter | solution.py:260
  603.1 266.3 %all-reduce.6 = f32[256,5120]{1,0:T(8,128)} all-reduce(bf16[256,5120]{1,0:T(8,128)(2,1)} %reduce-scatter.3.cloned.1.call-done), channel_id=1, replica_groups=mesh['dp'=8,'seq'=4] {'dp'}, use_global_device_ids=true, to_apply=%region_17.18 | all-reduce | flops 1310720 | bytes 7864320 | tf_op jit(solution)/shard_map/psum | solution.py:266
  874.4 116.1 %all-reduce.5.cloned.1.call-done = (f32[1024,1024]{0,1:T(8,128)}, f32[1024,1024]{0,1:T(8,128)}) async-done(((f32[1024,1024]{0,1:T(8,128)}, f32[1024,1024]{0,1:T(8,128)}), (f32[1024,1024]{0,1:T(8,128)}, f32[1024,1024]{0,1:T(8,128)})) %all-reduce.5.cloned.1.call-update) | async-done | bytes 8388624 | tf_op jit(solution)/shard_map/psum | solution.py:266
  (263 shorter events, 191.0 us)
Async XLA Ops:
  7.2 23.5 %copy-start.28 = (bf16[1024]{0:T(1024)(128)(2,1)S(1)}, bf16[1024]{0:T(1024)(128)(2,1)}, u32[]{:S(2)}) copy-start(bf16[1024]{0:T(1024)(128)(2,1)} %param.36) | copy-start | bytes 6148
  7.2 23.5 %copy-start.29 = (bf16[1024]{0:T(1024)(128)(2,1)S(1)}, bf16[1024]{0:T(1024)(128)(2,1)}, u32[]{:S(2)}) copy-start(bf16[1024]{0:T(1024)(128)(2,1)} %param.37) | copy-start | bytes 6148
  7.2 41.5 %all-gather.9.cloned.1.call-start = ((), (), s32[]{:S(2)}) async-start(), calls=%async_computation.7 | async-start | bytes 2621440 | tf_op jit(solution)/shard_map/all_gather | solution.py:147
  8.0 58.9 %all-gather.7.cloned.1.call-start = ((), (), s32[]{:S(2)}) async-start(), calls=%async_computation.6 | async-start | bytes 2621440 | tf_op jit(solution)/shard_map/all_gather | solution.py:146
  8.7 82.4 %all-gather.11.cloned.1.call-start = ((), (), s32[]{:S(2)}) async-start(), calls=%async_computation.8 | async-start | bytes 2621440 | tf_op jit(solution)/shard_map/all_gather | solution.py:148
  9.4 198.1 %all-gather.13.cloned.1.call-start = ((), (), s32[]{:S(2)}) async-start(), calls=%async_computation.9 | async-start | bytes 2621440 | tf_op jit(solution)/shard_map/all_gather | solution.py:149
  10.0 221.0 %all-gather.15.cloned.1.call-start = ((), (), s32[]{:S(2)}) async-start(), calls=%async_computation.10 | async-start | bytes 10485760 | tf_op jit(solution)/shard_map/all_gather | solution.py:151
  10.6 13.1 %collective-permute-start = (bf16[256,1024]{1,0:T(8,128)(2,1)S(1)}, bf16[256,1024]{1,0:T(8,128)(2,1)S(1)}, u32[]{:S(2)}, u32[]{:S(2)}) collective-permute-start(bf16[256,1024]{1,0:T(8,128)(2,1)S(1)} %copy-done.16), channel_id=1, source_target_pairs={{0,1},{1,2},{2,3},{3,0},{4,5},{5,6},{6,7},{7,4},{8,9},{9,10},{10,1... | collective-permute-start | bytes 1572872 | tf_op jit(solution)/shard_map/ppermute | solution.py:129
  11.2 19.7 %collective-permute-start.2 = (bf16[256,1024]{1,0:T(8,128)(2,1)S(1)}, bf16[256,1024]{1,0:T(8,128)(2,1)S(1)}, u32[]{:S(2)}, u32[]{:S(2)}) collective-permute-start(bf16[256,1024]{1,0:T(8,128)(2,1)S(1)} %copy-done.16), channel_id=1, source_target_pairs={{1,0},{2,1},{3,2},{0,3},{5,4},{6,5},{7,6},{4,7},{9,8},{10,9},{11,1... | collective-permute-start | bytes 1572872 | tf_op jit(solution)/shard_map/ppermute | solution.py:133
  23.8 18.7 %collective-permute-start.1 = (bf16[256,1024]{1,0:T(8,128)(2,1)S(1)}, bf16[256,1024]{1,0:T(8,128)(2,1)S(1)}, u32[]{:S(2)}, u32[]{:S(2)}) collective-permute-start(bf16[256,1024]{1,0:T(8,128)(2,1)S(1)} %collective-permute-done), channel_id=1, source_target_pairs={{0,1},{1,2},{2,3},{3,0},{4,5},{5,6},{6,7},{7,4},{8,9},{9,10},{10,1... | collective-permute-start | bytes 1572872 | tf_op jit(solution)/shard_map/ppermute | solution.py:129
  48.7 177.0 %copy-start.19 = (f32[1024]{0:T(1024)}, f32[1024]{0:T(1024)S(1)}, u32[]{:S(2)}) copy-start(f32[1024]{0:T(1024)S(1)} %convert_add_fusion.1) | copy-start | bytes 12292
  100.1 83.5 %all-to-all-start = ((bf16[1,512,3,1024]{1,2,0,3:T(4,128)(2,1)}), bf16[1,512,3,1024]{1,2,0,3:T(4,128)(2,1)}, u32[]{:S(2)}, u32[]{:S(2)}) async-start(bf16[1,512,3,1024]{1,2,0,3:T(4,128)(2,1)} %copy.80), calls=%async_computation | async-start | bytes 8388608 | tf_op jit(solution)/shard_map/all_to_all | solution.py:183
  105.2 163.2 %all-gather.17.cloned.1.call-start = ((), (), s32[]{:S(2)}) async-start(), calls=%async_computation.11 | async-start | bytes 10485760 | tf_op jit(solution)/shard_map/all_gather | solution.py:152
  186.6 20.7 %copy-start.33 = (bf16[1024]{0:T(1024)(128)(2,1)S(1)}, bf16[1024]{0:T(1024)(128)(2,1)}, u32[]{:S(2)}) copy-start(bf16[1024]{0:T(1024)(128)(2,1)} %param.43) | copy-start | bytes 6148
  186.7 20.7 %copy-start.27 = (bf16[4096]{0:T(1024)(128)(2,1)S(1)}, bf16[4096]{0:T(1024)(128)(2,1)}, u32[]{:S(2)}) copy-start(bf16[4096]{0:T(1024)(128)(2,1)} %param.40) | copy-start | bytes 24580
  186.7 20.7 %copy-start.34 = (bf16[1024]{0:T(1024)(128)(2,1)S(1)}, bf16[1024]{0:T(1024)(128)(2,1)}, u32[]{:S(2)}) copy-start(bf16[1024]{0:T(1024)(128)(2,1)} %param.41) | copy-start | bytes 6148
  186.7 20.8 %copy-start.35 = (bf16[1024]{0:T(1024)(128)(2,1)S(1)}, bf16[1024]{0:T(1024)(128)(2,1)}, u32[]{:S(2)}) copy-start(bf16[1024]{0:T(1024)(128)(2,1)} %param.44) | copy-start | bytes 6148
  186.7 20.8 %copy-start.36 = (bf16[1024]{0:T(1024)(128)(2,1)S(1)}, bf16[1024]{0:T(1024)(128)(2,1)}, u32[]{:S(2)}) copy-start(bf16[1024]{0:T(1024)(128)(2,1)} %param.45) | copy-start | bytes 6148
  203.0 22.7 %all-to-all-start.1 = ((bf16[4,512,256]{1,2,0:T(8,128)(2,1)}), bf16[4,512,256]{1,2,0:T(8,128)(2,1)}, u32[]{:S(2)}, u32[]{:S(2)}) async-start(bf16[4,512,256]{1,2,0:T(8,128)(2,1)} %get-tuple-element.79), calls=%async_computation.1 | async-start | bytes 2097152 | tf_op jit(solution)/shard_map/all_to_all | solution.py:185
  207.3 310.5 %reduce-scatter.5.cloned.1.call-start = ((), (), s32[]{:S(2)}) async-start(), calls=%async_computation.13 | async-start | bytes 20971520 | tf_op jit(solution)/shard_map/reduce_scatter | solution.py:248
  363.2 30.4 %all-to-all-start.2 = ((bf16[4,2,65536]{2,1,0:T(2,128)(2,1)}), bf16[4,2,65536]{2,1,0:T(2,128)(2,1)}, u32[]{:S(2)}, u32[]{:S(2)}) async-start(bf16[4,2,65536]{2,1,0:T(2,128)(2,1)} %reshape.330), calls=%async_computation.2 | async-start | bytes 2097152 | tf_op jit(solution)/shard_map/all_to_all | solution.py:219
  435.5 59.0 %all-to-all-start.3 = ((bf16[4,512,3,256]{1,3,2,0:T(8,128)(2,1)}), bf16[4,512,3,256]{1,3,2,0:T(8,128)(2,1)S(1)}, u32[]{:S(2)}, u32[]{:S(2)}) async-start(bf16[4,512,3,256]{1,3,2,0:T(8,128)(2,1)} %get-tuple-element.81), calls=%async_computation.3 | async-start | bytes 6291456 | tf_op jit(solution)/shard_map/all_to_all | solution.py:227
  439.3 163.8 %reduce-scatter.3.cloned.1.call-start = ((), (), s32[]{:S(2)}) async-start(), calls=%async_computation.12 | async-start | bytes 13107200 | tf_op jit(solution)/shard_map/reduce_scatter | solution.py:260
  517.7 472.9 %all-reduce.5.cloned.1.call-start = ((), (), s32[]{:S(2)}) async-start(), calls=%async_computation.14 | async-start | bytes 16777216 | tf_op jit(solution)/shard_map/psum | solution.py:266
  (35 other events, 182.9 us)
Sparse Core Ops, SparseCore 0:
  9.6 32.9 all-gather.8
  44.2 22.6 all-gather.6
  68.5 22.5 all-gather.10
  92.5 27.7 all-gather.12
  121.7 83.4 all-gather.14
  206.6 61.7 all-gather.16
  326.1 154.4 reduce-scatter.4
  517.8 85.2 reduce-scatter.2
  608.3 382.1 all-reduce.4
